TPU v7x, 32 devices: a whole 2x2x4 slice. The times are simulated.
32 devices in a mesh: group: 2 (over y), beam: 4 (over z), fft: 2 (over x), sub: 2 (over core).
Axes of the slice: x: 2, y: 2, z: 4, core: 2. Of those that a mesh axis runs over, the one named last changes fastest.
Arguments:
- uv_grid: float32 [8, 2, 2048, 2048], P(('group', 'beam'), None, ('fft', 'sub')), parts along dimension 0, may hold values from -6 to 6
- beam_gain: float32 [8, 512, 512], P(('group', 'beam'), ('fft', 'sub')), parts along dimension 0, may hold values from 0.1 to 1
- sub_pixel: float32 [8, 2], P(('group', 'beam')), parts along dimension 0, may hold values from 0 to 1
- intersection_tiles: int32 [8, 4], P('group'), parts along dimension 0, may hold values from 0 to 7, as said below
- tile_offsets: int32 [8, 4, 2], P(('group', 'beam')), parts along dimension 0, may hold values from 0 to 252
Outputs:
- sky: float32 [16, 256, 256], P(('group', 'beam'), ('fft', 'sub')), parts along dimension 0
There are 2 independent parts, one for each index of `group`. A program takes and returns all parts, laid end to end along the dimension named above; each array names one. Nothing has to cross between parts.
Inputs may be any that keep to these rules, and one draw needn't show every extreme that they name: `intersection_tiles`: each row names 4 distinct sky tiles; sky tile t belongs to owner t // 2, and the tiles of beam b belong to owners b - 1 to b + 2 taken modulo the number of owners, with at most 2 of them on one owner.
All inputs are finite; a program needn't handle non-finite values.
Results may differ from a plain program's by a relative error of at most 0.0037.
Values may be sent and summed in bfloat16 or wider, within the bound.
A program may use at most 64 MiB of HBM per device.

v0:
```python
import functools

import jax
import jax.numpy as jnp
import ml_dtypes
import numpy as np
from jax import lax
from jax.experimental import pallas as pl
from jax.experimental.pallas import tpu as pltpu
from jax.sharding import PartitionSpec as P

S = 256
TILE_DEV = 2
RADIX = 4
HOPS = (1, -1, 2)
MESH = pl.DeviceIdType.MESH
F32 = jnp.float32
BF16 = jnp.bfloat16


def turns(rows, cols, length):
    angle = np.mod(np.outer(rows, cols), length) * (2.0 * np.pi / length)
    return np.cos(angle), np.sin(angle)


def column_tables(length, window):
    fold = length // RADIX
    per = window // RADIX
    tables = []
    for c in range(RADIX):
        cos, sin = turns(np.arange(fold), RADIX * np.arange(per) + c - window // 2, length)
        tables.append(np.concatenate([cos, sin], axis=1))
    full = np.stack(tables).astype(np.float32)
    high = full.astype(ml_dtypes.bfloat16)
    low = (full - high.astype(np.float32)).astype(ml_dtypes.bfloat16)
    return np.stack([high, low])


def row_tables(length, window, rows):
    cos, sin = turns(np.arange(window) - window // 2, np.arange(rows), length)
    return np.stack([cos, sin]).astype(np.float32).astype(ml_dtypes.bfloat16)


def near(a):
    return (1.5 * a - 2.5) * a * a + 1.0


def far(a):
    return ((-0.5 * a + 2.5) * a - 4.0) * a + 2.0


def taps(frac):
    return far(1.0 + frac), near(frac), near(1.0 - frac), far(2.0 - frac)


def kernel(
    groups, quarter, step, shift_ref, tiles_ref, offs_ref, gain_ref, uv_ref, col_hbm, row_hbm, out_ref,
    buf, col_ref, row_ref, table, spec, gall, hsend, hrecv, psend, precv, filt, squares, crops,
    nsend, nrecv, znsend, znrecv, zdsend, zdrecv,
    load_sems, send_sems, recv_sems,
):
    chip, core = lax.axis_index("fft"), lax.axis_index("sub")
    chips, cores = lax.axis_size("fft"), lax.axis_size("sub")
    me = chip * cores + core
    owner = lax.axis_index("beam")
    owners = lax.axis_size("beam")
    rows, length = buf.shape[1], buf.shape[2]
    fold = length // RADIX
    window = gain_ref.shape[2]
    per = window // RADIX
    wide = window // groups
    side = S // groups
    count = offs_ref.shape[2]
    chunks = rows // step
    padded = crops.shape[2]

    def load(i):
        span = pl.ds(pl.multiple_of(i * step, step), step)
        return pltpu.make_async_copy(uv_ref.at[0, :, span], buf.at[:, span], load_sems.at[i])

    col_load = pltpu.make_async_copy(col_hbm, col_ref, load_sems.at[chunks])
    row_load = pltpu.make_async_copy(row_hbm, row_ref, load_sems.at[chunks + 1])
    col_load.start()
    for i in range(chunks):
        load(i).start()
    row_load.start()

    def beam(hop):
        return {"beam": lax.rem(owner + hop + owners, owners)}

    peers = []
    for a in list(range(1, chips)) + [0]:
        for e in range(cores):
            if a or e:
                to = (lax.rem(chip + a, chips), lax.rem(core + e, cores))
                frm = (lax.rem(chip - a + chips, chips), lax.rem(core - e + cores, cores))
                peers.append((
                    {"fft": to[0], "sub": to[1]}, to[0] * cores + to[1], frm[0] * cores + frm[1]))
    lanes = len(peers)
    shared = 2 * lanes + 1

    barrier = pltpu.get_barrier_semaphore()
    for device, _, _ in peers:
        pl.semaphore_signal(barrier, inc=1, device_id=device, device_id_type=MESH)
    for hop in HOPS:
        pl.semaphore_signal(barrier, inc=1, device_id=beam(-hop), device_id_type=MESH)

    def remote(src, dst, index, device):
        return pltpu.make_async_remote_copy(
            src_ref=src, dst_ref=dst, send_sem=send_sems.at[index], recv_sem=recv_sems.at[index],
            device_id=device, device_id_type=MESH)

    def natural(place):
        return RADIX * jnp.bitwise_and(place, per - 1) + lax.shift_right_logical(place, per.bit_length() - 1)

    own_rows = gain_ref.shape[1]

    def rows_of(member):
        return gall.at[pl.ds(pl.multiple_of(member * own_rows, own_rows), own_rows)]

    def at(a, e):
        other = lax.rem(chip + a + chips, chips), lax.rem(core + e + cores, cores)
        return {"fft": other[0], "sub": other[1]}, other[0] * cores + other[1]

    def slot_of(a, e):
        return a * cores + e

    pl.semaphore_wait(barrier, lanes + len(HOPS))
    gain_copies = []
    for a in list(range(1, chips)) + [0]:
        for e in range(cores):
            if (a == 0) != (e == 0):
                gain_copies.append(remote(gain_ref.at[0], rows_of(me), slot_of(a, e), at(a, e)[0]))
    for c in gain_copies:
        c.start()
    gall[pl.ds(pl.multiple_of(me * own_rows, own_rows), own_rows), :] = gain_ref[0]

    down = taps(shift_ref[0, 0])
    across = taps(shift_ref[0, 1])

    def filter_rows(x):
        total = down[0] * x
        for d in range(1, 4):
            total += down[d] * pltpu.roll(x, window - d, 0)
        return total

    def filter_columns(x):
        total = across[0] * x
        for d in range(1, 4):
            total += across[d] * pltpu.roll(x, padded - d, 1)
        return total[:, :S]

    def columns(i, carry):
        load(i).wait()
        span = pl.ds(pl.multiple_of(i * step, step), step)
        a = [buf[0, span, j * fold:(j + 1) * fold] for j in range(RADIX)]
        b = [buf[1, span, j * fold:(j + 1) * fold] for j in range(RADIX)]
        ap, am, aq, an = a[0] + a[2], a[0] - a[2], a[1] + a[3], a[1] - a[3]
        bp, bm, bq, bn = b[0] + b[2], b[0] - b[2], b[1] + b[3], b[1] - b[3]
        folded = (
            (ap + aq, bp + bq),
            (am - bn, bm + an),
            (ap - aq, bp - bq),
            (am + bn, bm - an),
        )
        for c in range(RADIX):
            z = jnp.concatenate(folded[c], axis=0)
            high = z.astype(BF16)
            low = (z - high.astype(F32)).astype(BF16)
            out = jnp.dot(high, col_ref[0, c], preferred_element_type=F32)
            out += jnp.dot(low, col_ref[0, c], preferred_element_type=F32)
            out += jnp.dot(high, col_ref[1, c], preferred_element_type=F32)
            real = (out[:step, :per] - out[step:, per:]).astype(BF16)
            imag = (out[:step, per:] + out[step:, :per]).astype(BF16)
            for g in range(c * per // wide, (c + 1) * per // wide):
                at = g * wide - c * per
                spec[g, span] = real[:, at:at + wide]
                spec[g, pl.ds(pl.multiple_of(rows + i * step, step), step)] = imag[:, at:at + wide]
        return carry

    col_load.wait()
    lax.fori_loop(0, chunks // 2, columns, 0)
    row_load.wait()
    cos = row_ref[0].astype(F32)
    sin = row_ref[1].astype(F32)
    if quarter:
        turn = jnp.bitwise_and(me * lax.broadcasted_iota(jnp.int32, (window, 1), 0), 3)
        plus = jnp.where(turn == 0, 1.0, jnp.where(turn == 2, -1.0, 0.0))
        cross = jnp.where(turn == 1, 1.0, jnp.where(turn == 3, -1.0, 0.0))
        cos, sin = plus * cos - cross * sin, cross * cos + plus * sin
    table[:, :rows] = cos.astype(BF16)
    table[:, rows:] = (-sin).astype(BF16)
    lax.fori_loop(chunks // 2, chunks, columns, 0)

    def share(member):
        return jnp.dot(table[...], spec[member], preferred_element_type=F32) * (1.0 / length)

    base = lanes + 1
    part_copies = []
    core_copies = {}
    for e in range(1, cores):
        for a in list(range(1, chips)) + [0]:
            i = (e - 1) * chips + a
            hsend[i] = share(at(a, e)[1]).astype(BF16)
            c = remote(hsend.at[i], hrecv.at[i], base + i, at(0, e)[0])
            c.start()
            core_copies[a, e] = c
    base += (cores - 1) * chips
    for a in range(1, chips):
        total = share(at(a, 0)[1])
        for e in range(1, cores):
            core_copies[a, e].wait_recv()
            total += hrecv[(e - 1) * chips + a].astype(F32)
        psend[a - 1] = total.astype(BF16)
        c = remote(psend.at[a - 1], precv.at[a - 1], base + a - 1, at(a, 0)[0])
        c.start()
        part_copies.append(c)
    for a in range(1, chips):
        remote(gain_ref.at[0], rows_of(at(-a, 0)[1]), slot_of(a, 0), at(a, 0)[0]).wait_recv()
        for e in range(1, cores):
            c = remote(rows_of(at(-a, 0)[1]), rows_of(at(-a, 0)[1]), slot_of(a, e), at(0, e)[0])
            c.start()
            gain_copies.append(c)
    image = share(me)
    for e in range(1, cores):
        core_copies[0, e].wait_recv()
        image += hrecv[(e - 1) * chips].astype(F32)

    column = natural(lax.broadcasted_iota(jnp.int32, (window, 1), 0))
    target = lax.broadcasted_iota(jnp.int32, (window, padded), 1)
    for k in range(count):
        crops[k] = jnp.where(target == column - offs_ref[0, 1, k], 1.0, 0.0).astype(BF16)

    for a in range(chips):
        for e in range(1, cores):
            frm = at(-a, -e)[1]
            remote(rows_of(frm), rows_of(frm), slot_of(a, e), at(0, e)[0]).wait_recv()
    source = lax.broadcasted_iota(jnp.int32, (window, wide), 0)
    order = jnp.where(source == natural(me * wide + lax.broadcasted_iota(jnp.int32, (1, wide), 1)), 1.0, 0.0)
    order = order.astype(BF16)
    gain = gall[...]
    high = gain.astype(BF16)
    low = (gain - high.astype(F32)).astype(BF16)
    beam_gain = jnp.dot(high, order, preferred_element_type=F32) + jnp.dot(low, order, preferred_element_type=F32)

    def owed(pieces, hop, slot):
        tile = lax.rem(owner + hop + owners, owners) * TILE_DEV + slot
        total = jnp.zeros((side, S), F32)
        for k in range(count):
            total += jnp.where(tiles_ref[owner, k] == tile, 1.0, 0.0) * pieces[k]
        return total

    pieces = []
    for q in range(window // 128):
        g = gall[:, q * 128:(q + 1) * 128]
        squares[q] = filter_rows(g * g)
    place = lax.broadcasted_iota(jnp.int32, (window, 1), 0)
    for k in range(count):
        den = jnp.concatenate(
            [squares[q, pl.ds(offs_ref[0, 0, k] + me * side, side), :] for q in range(window // 128)], axis=1)
        high = den.astype(BF16)
        low = (den - high.astype(F32)).astype(BF16)
        crop = jnp.where(target == place - offs_ref[0, 1, k], 1.0, 0.0).astype(BF16)
        got = jnp.dot(jnp.concatenate([high, low], axis=0), crop, preferred_element_type=F32)
        pieces.append(filter_columns(got[:side] + got[side:]))
    base = shared
    beam_copies = []
    for h, hop in enumerate(HOPS):
        for slot in range(TILE_DEV):
            zdsend[h, slot] = owed(pieces, hop, slot).astype(BF16)
        c = remote(zdsend.at[h], zdrecv.at[h], base + h, beam(hop))
        c.start()
        beam_copies.append(c)
    dens = [owed(pieces, 0, slot) for slot in range(TILE_DEV)]

    for i, c in enumerate(part_copies):
        c.wait_recv()
        image += precv[i].astype(F32)
    filt[...] = filter_rows(beam_gain * image)
    base = shared + 2 * len(HOPS)
    num_copies = []
    for i, (device, to, _) in enumerate(peers):
        for k in range(count):
            nsend[to, k] = filt[pl.ds(offs_ref[0, 0, k] + to * side, side), :].astype(BF16)
        c = remote(nsend.at[to], nrecv.at[me], base + i, device)
        c.start()
        num_copies.append(c)
    for k in range(count):
        nrecv[me, k] = filt[pl.ds(offs_ref[0, 0, k] + me * side, side), :].astype(BF16)
    for i, (device, to, frm) in enumerate(peers):
        remote(nsend.at[to], nrecv.at[frm], base + i, device).wait_recv()

    pieces = []
    for k in range(count):
        num = jnp.concatenate([nrecv[g, k] for g in range(groups)], axis=1)
        pieces.append(filter_columns(jnp.dot(num, crops[k], preferred_element_type=F32)))
    base = shared + len(HOPS)
    for h, hop in enumerate(HOPS):
        for slot in range(TILE_DEV):
            znsend[h, slot] = owed(pieces, hop, slot).astype(BF16)
        c = remote(znsend.at[h], znrecv.at[h], base + h, beam(hop))
        c.start()
        beam_copies.append(c)
    nums = [owed(pieces, 0, slot) for slot in range(TILE_DEV)]
    for c in beam_copies:
        c.wait_recv()
    for slot in range(TILE_DEV):
        num, den = nums[slot], dens[slot]
        for h in range(len(HOPS)):
            num += znrecv[h, slot].astype(F32)
            den += zdrecv[h, slot].astype(F32)
        out_ref[slot] = num / jnp.maximum(den, 0.5)
    for c in gain_copies + list(core_copies.values()) + part_copies + num_copies + beam_copies:
        c.wait_send()


def body(uv_grid, beam_gain, sub_pixel, intersection_tiles, tile_offsets):
    groups = lax.axis_size(("fft", "sub"))
    rows = uv_grid.shape[2]
    length = uv_grid.shape[3]
    own_rows = beam_gain.shape[1]
    window = beam_gain.shape[2]
    wide = window // groups
    side = S // groups
    count = tile_offsets.shape[1]
    quarter = RADIX * rows == length
    if quarter:
        row_table = jnp.asarray(row_tables(length, window, rows))
    else:
        member = lax.axis_index("fft") * lax.axis_size("sub") + lax.axis_index("sub")
        freq = member * rows + jnp.arange(rows, dtype=jnp.int32)
        place = jnp.arange(window, dtype=jnp.int32) - window // 2
        angle = jnp.mod(place[:, None] * freq[None, :], length).astype(F32) * (2.0 * np.pi / length)
        row_table = jnp.stack([jnp.cos(angle), jnp.sin(angle)]).astype(BF16)
    col_table = jnp.asarray(column_tables(length, window))
    step = min(128, rows)
    vmem = pl.BlockSpec(memory_space=pltpu.VMEM)
    smem = pl.BlockSpec(memory_space=pltpu.SMEM)
    anywhere = pl.BlockSpec(memory_space=pl.ANY)
    hops = len(HOPS)
    copies = 3 * (groups - 1) + 1 + 2 * hops
    chips, cores = lax.axis_size("fft"), lax.axis_size("sub")
    left = (groups, count, side, wide)
    owed = (hops, TILE_DEV, side, S)
    return pl.pallas_call(
        functools.partial(kernel, groups, quarter, step),
        out_shape=jax.ShapeDtypeStruct((TILE_DEV, side, S), F32),
        in_specs=[smem, smem, smem, vmem, anywhere, anywhere, anywhere],
        out_specs=vmem,
        scratch_shapes=[
            pltpu.VMEM((2, rows, length), F32),
            pltpu.VMEM(col_table.shape, BF16),
            pltpu.VMEM(row_table.shape, BF16),
            pltpu.VMEM((window, 2 * rows), BF16),
            pltpu.VMEM((groups, 2 * rows, wide), BF16),
            pltpu.VMEM((window, window), F32),
            pltpu.VMEM(((cores - 1) * chips, window, wide), BF16),
            pltpu.VMEM(((cores - 1) * chips, window, wide), BF16),
            pltpu.VMEM((chips - 1, window, wide), BF16),
            pltpu.VMEM((chips - 1, window, wide), BF16),
            pltpu.VMEM((window, wide), F32),
            pltpu.VMEM((window // 128, window, 128), F32),
            pltpu.VMEM((count, window, S + 128), BF16),
            pltpu.VMEM(left, BF16),
            pltpu.VMEM(left, BF16),
            pltpu.VMEM(owed, BF16),
            pltpu.VMEM(owed, BF16),
            pltpu.VMEM(owed, BF16),
            pltpu.VMEM(owed, BF16),
            pltpu.SemaphoreType.DMA((rows // step + 2,)),
            pltpu.SemaphoreType.DMA((copies,)),
            pltpu.SemaphoreType.DMA((copies,)),
        ],
        compiler_params=pltpu.CompilerParams(collective_id=0, has_side_effects=True),
    )(sub_pixel, intersection_tiles, jnp.swapaxes(tile_offsets, 1, 2), beam_gain, uv_grid, col_table, row_table)


def solution(mesh):
    placed = (
        P(("group", "beam"), None, ("fft", "sub"), None),
        P(("group", "beam"), ("fft", "sub"), None),
        P(("group", "beam"), None),
        P("group", None),
        P(("group", "beam"), None, None),
    )
    return jax.shard_map(
        body,
        mesh=mesh,
        in_specs=placed,
        out_specs=P(("group", "beam"), ("fft", "sub"), None),
        check_vma=False,
    )
```

profile of v0, /device:TPU:0, one launch (start us, length us, event | category | flops | bytes accessed | tf_op | source)
XLA Modules:
  0.0 32.9 jit_solution(9062813118644731230)
XLA Ops:
  0.0 31.3 %shard_map.73 = f32[2,64,256]{2,1,0:T(8,128)} custom-call(f32[1,2]{1,0:T(1,128)} %shift_ref.1, s32[4,4]{1,0:T(4,128)} %tiles_ref.1, s32[1,2,4]{2,1,0:T(2,128)} %bitcast.1, f32[1,128,512]{2,1,0:T(8,128)} %gain_ref.1, f32[1,2,512,2048]{3,2,1,0:T(8,128)} %uv_ref.1, bf16[2,4,512,256]{3,2,1,0:T(8,128)(2,1)} %constant.5.clone.col_hbm, ...), custom_call_target="tpu_custom_call" | custom-call | tf_op jit(solution)/shard_map/pallas_call | solution.py:345
  31.3 1.6 %copy.9 = f32[2,64,256]{2,1,0:T(8,128)} copy(f32[2,64,256]{2,1,0:T(8,128)} %shard_map.73) | data formatting | bytes 262144
where the time goes:
time: 33.1 us; the launch traced here: 32.9 us
  Pallas kernels  31.3 us (95%)
  local copies, waits for them, and re-layouts  1.57 us (5%)
    pallas_call x1, Pallas kernels, body(): pl.pallas_call(functools.partial(kernel, groups, quarter, step), out_shap...  31.3 us
    unnamed x1, local copies, waits for them, and re-layouts  1.57 us

commit v1 on v0

v1 whole, which is shorter than its diff:
```python
import functools

import jax
import jax.numpy as jnp
import ml_dtypes
import numpy as np
from jax import lax
from jax.experimental import pallas as pl
from jax.experimental.pallas import tpu as pltpu
from jax.sharding import PartitionSpec as P

S = 256
TILE_DEV = 2
RADIX = 4
HOPS = (2, 1, -1)
PARTS = 2
LEVELS = 32000.0
LANES = 128
MESH = pl.DeviceIdType.MESH
F32 = jnp.float32
BF16 = jnp.bfloat16


def turns(rows, cols, length):
    angle = np.mod(np.outer(rows, cols), length) * (2.0 * np.pi / length)
    return np.cos(angle), np.sin(angle)


def column_tables(length, window):
    fold = length // RADIX
    per = window // RADIX
    tables = []
    for c in range(RADIX):
        cos, sin = turns(np.arange(fold), RADIX * np.arange(per) + c - window // 2, length)
        tables.append(np.concatenate([cos, sin], axis=1))
    full = np.stack(tables).astype(np.float32)
    high = full.astype(ml_dtypes.bfloat16)
    low = (full - high.astype(np.float32)).astype(ml_dtypes.bfloat16)
    return np.stack([high, low])


def row_tables(length, window, rows):
    cos, sin = turns(np.arange(window) - window // 2, np.arange(rows), length)
    return np.stack([cos, sin]).astype(np.float32).astype(ml_dtypes.bfloat16)


def near(a):
    return (1.5 * a - 2.5) * a * a + 1.0


def far(a):
    return ((-0.5 * a + 2.5) * a - 4.0) * a + 2.0


def taps(frac):
    return far(1.0 + frac), near(frac), near(1.0 - frac), far(2.0 - frac)


def kernel(
    quarter, step, shift_ref, tiles_ref, offs_ref, gain_hbm, uv_ref, col_hbm, row_hbm, out_ref,
    buf, col_ref, row_ref, table, spec, own, gall, filt, squares, mats, pieces, psend, precv,
    xsend, xrecv, zsend, zrecv, dsend, drecv,
    load_sems, gsems, grecv, csems, crecv, xsems, xrsems, zsems, zrsems, dsems, drsems,
):
    chip, core = lax.axis_index("fft"), lax.axis_index("sub")
    chips, cores = lax.axis_size("fft"), lax.axis_size("sub")
    me = chip * cores + core
    owner = lax.axis_index("beam")
    owners = lax.axis_size("beam")
    rows, length = buf.shape[1], buf.shape[2]
    fold = length // RADIX
    own_rows, window = own.shape
    per = window // RADIX
    side = pieces.shape[3]
    count = offs_ref.shape[2]
    chunks = rows // step
    parts = xsend.shape[0]
    cut = side // parts

    def load(i):
        span = pl.ds(pl.multiple_of(i * step, step), step)
        return pltpu.make_async_copy(uv_ref.at[0, :, span], buf.at[:, span], load_sems.at[i])

    gain_load = pltpu.make_async_copy(gain_hbm.at[0], own, load_sems.at[chunks])
    col_load = pltpu.make_async_copy(col_hbm, col_ref, load_sems.at[chunks + 1])
    row_load = pltpu.make_async_copy(row_hbm, row_ref, load_sems.at[chunks + 2])
    gain_load.start()
    col_load.start()
    for i in range(chunks):
        load(i).start()
    row_load.start()

    def beam(hop):
        return {"beam": lax.rem(owner + hop + owners, owners)}

    def at(a, e):
        other = lax.rem(chip + a + chips, chips), lax.rem(core + e + cores, cores)
        return {"fft": other[0], "sub": other[1]}, other[0] * cores + other[1]

    barrier = pltpu.get_barrier_semaphore()
    for a in range(chips):
        for e in range(cores):
            if a or e:
                pl.semaphore_signal(barrier, inc=1, device_id=at(a, e)[0], device_id_type=MESH)
    for hop in HOPS:
        pl.semaphore_signal(barrier, inc=1, device_id=beam(-hop), device_id_type=MESH)

    def remote(src, dst, send, recv, device):
        return pltpu.make_async_remote_copy(
            src_ref=src, dst_ref=dst, send_sem=send, recv_sem=recv, device_id=device, device_id_type=MESH)

    def natural(place):
        return RADIX * jnp.bitwise_and(place, per - 1) + lax.shift_right_logical(place, per.bit_length() - 1)

    def rows_of(member):
        return gall.at[pl.ds(pl.multiple_of(member * own_rows, own_rows), own_rows)]

    def gain_copy(a, e, member):
        rel = a * cores + e
        to = at(a, 0)[0] if e == 0 else at(0, e)[0]
        return remote(rows_of(member), rows_of(member), gsems.at[rel], grecv.at[rel], to)

    place = lax.broadcasted_iota(jnp.int32, (window, 1), 0)
    column = natural(lax.broadcasted_iota(jnp.int32, (1, window), 1))
    order = jnp.where(place == column, 1.0, 0.0).astype(BF16)
    gain_load.wait()
    gain = own[...]
    high = gain.astype(BF16)
    low = (gain - high.astype(F32)).astype(BF16)
    gain = jnp.dot(high, order, preferred_element_type=F32) + jnp.dot(low, order, preferred_element_type=F32)
    gall[pl.ds(pl.multiple_of(me * own_rows, own_rows), own_rows), :] = (gain * LEVELS + 0.5).astype(jnp.int16)

    pl.semaphore_wait(barrier, chips * cores - 1 + len(HOPS))
    gain_copies = [gain_copy(a, 0, me) for a in range(1, chips)] + [gain_copy(0, e, me) for e in range(1, cores)]
    for c in gain_copies:
        c.start()

    down = taps(shift_ref[0, 0])
    across = taps(shift_ref[0, 1])

    def filter_rows(x):
        total = down[0] * x
        for d in range(1, 4):
            total += down[d] * pltpu.roll(x, window - d, 0)
        return total

    def rounded(tap):
        return jnp.full((1, S), tap, F32).astype(BF16).astype(F32)

    tops = [rounded(tap) for tap in across]
    rests = [tap - top for tap, top in zip(across, tops)]
    source = natural(place) - lax.broadcasted_iota(jnp.int32, (window, S), 1)
    for k in range(count):
        gap = source - offs_ref[0, 1, k]
        top = jnp.zeros((window, S), F32)
        rest = top
        for d in range(4):
            hit = gap == d
            top = jnp.where(hit, tops[d], top)
            rest = jnp.where(hit, rests[d], rest)
        mats[0, k] = top.astype(BF16)
        mats[1, k] = rest.astype(BF16)

    def columns(i, carry):
        load(i).wait()
        span = pl.ds(pl.multiple_of(i * step, step), step)
        a = [buf[0, span, j * fold:(j + 1) * fold] for j in range(RADIX)]
        b = [buf[1, span, j * fold:(j + 1) * fold] for j in range(RADIX)]
        ap, am, aq, an = a[0] + a[2], a[0] - a[2], a[1] + a[3], a[1] - a[3]
        bp, bm, bq, bn = b[0] + b[2], b[0] - b[2], b[1] + b[3], b[1] - b[3]
        folded = (
            (ap + aq, bp + bq),
            (am - bn, bm + an),
            (ap - aq, bp - bq),
            (am + bn, bm - an),
        )
        for c in range(RADIX):
            z = jnp.concatenate(folded[c], axis=0)
            high = z.astype(BF16)
            low = (z - high.astype(F32)).astype(BF16)
            out = jnp.dot(high, col_ref[0, c], preferred_element_type=F32)
            out += jnp.dot(low, col_ref[0, c], preferred_element_type=F32)
            out += jnp.dot(high, col_ref[1, c], preferred_element_type=F32)
            real = (out[:step, :per] - out[step:, per:]).astype(BF16)
            imag = (out[:step, per:] + out[step:, :per]).astype(BF16)
            spec[span, c * per:(c + 1) * per] = real
            spec[pl.ds(pl.multiple_of(rows + i * step, step), step), c * per:(c + 1) * per] = imag
        return carry

    col_load.wait()
    lax.fori_loop(0, chunks // 2, columns, 0)
    row_load.wait()
    cos = row_ref[0].astype(F32)
    sin = row_ref[1].astype(F32)
    if quarter:
        turn = jnp.bitwise_and(me * place, 3)
        plus = jnp.where(turn == 0, 1.0, jnp.where(turn == 2, -1.0, 0.0))
        cross = jnp.where(turn == 1, 1.0, jnp.where(turn == 3, -1.0, 0.0))
        cos, sin = plus * cos - cross * sin, cross * cos + plus * sin
    table[:, :rows] = cos.astype(BF16)
    table[:, rows:] = (-sin).astype(BF16)
    lax.fori_loop(chunks // 2, chunks - 1, columns, 0)
    for a in range(1, chips):
        frm = at(-a, 0)[1]
        gain_copy(a, 0, frm).wait_recv()
        for e in range(1, cores):
            c = gain_copy(a, e, frm)
            c.start()
            gain_copies.append(c)
    lax.fori_loop(chunks - 1, chunks, columns, 0)

    for a in range(chips):
        for e in range(1, cores):
            gain_copy(a, e, at(-a, -e)[1]).wait_recv()
    scale = 1.0 / (LEVELS * length)
    half = window // 2
    for q in range(2):
        image = jnp.dot(table[...], spec[:, q * half:(q + 1) * half], preferred_element_type=F32)
        image = filter_rows(image * (gall[:, q * half:(q + 1) * half].astype(F32) * scale))
        for j in range(half // LANES):
            filt[q * half // LANES + j] = image[:, j * LANES:(j + 1) * LANES]

    def cropped(ref, start, size):
        return jnp.concatenate([ref[q, pl.ds(start, size), :] for q in range(window // LANES)], axis=1)

    core_copies = []
    for k in range(count):
        left = cropped(filt, offs_ref[0, 0, k], S).astype(BF16)
        piece = jnp.dot(left, mats[0, k], preferred_element_type=F32)
        piece += jnp.dot(left, mats[1, k], preferred_element_type=F32)
        for a in range(chips):
            for e in range(cores):
                m = a * cores + e
                pieces[k, e, a] = piece[m * side:(m + 1) * side]
                psend[k, e, a] = piece[m * side:(m + 1) * side].astype(BF16)
        for e in range(1, cores):
            to = lax.rem(core + e, cores)
            c = remote(psend.at[k, to], precv.at[e - 1, k], csems.at[e - 1, k], crecv.at[e - 1, k], at(0, e)[0])
            c.start()
            core_copies.append(c)

    def owed(terms, hop, slot):
        tile = lax.rem(owner + hop + owners, owners) * TILE_DEV + slot
        total = jnp.where(tiles_ref[owner, 0] == tile, 1.0, 0.0) * terms[0]
        for k in range(1, count):
            total += jnp.where(tiles_ref[owner, k] == tile, 1.0, 0.0) * terms[k]
        return total

    for q in range(window // LANES):
        g = gall[:, q * LANES:(q + 1) * LANES].astype(F32) * (1.0 / LEVELS)
        squares[q] = filter_rows(g * g)
    terms = []
    for k in range(count):
        den = cropped(squares, offs_ref[0, 0, k] + me * side, side)
        high = den.astype(BF16)
        low = (den - high.astype(F32)).astype(BF16)
        both = jnp.dot(jnp.concatenate([high, low], axis=0), mats[0, k], preferred_element_type=F32)
        terms.append(both[:side] + both[side:] + jnp.dot(high, mats[1, k], preferred_element_type=F32))
    den_copies = []
    for h, hop in enumerate(HOPS):
        for slot in range(TILE_DEV):
            dsend[h, slot] = owed(terms, hop, slot).astype(BF16)
        c = remote(dsend.at[h], drecv.at[h], dsems.at[h], drsems.at[h], beam(hop))
        c.start()
        den_copies.append(c)
    dens = [owed(terms, 0, slot) for slot in range(TILE_DEV)]

    for c in core_copies:
        c.wait_recv()

    def summed(k, to, p):
        span = slice(p * cut, (p + 1) * cut)
        total = pieces[k, core, to, span]
        for e in range(1, cores):
            total += precv[e - 1, k, to, span].astype(F32)
        return total

    x_copies = []
    for p in range(parts):
        for a in range(1, chips):
            to = lax.rem(chip + a, chips)
            for k in range(count):
                xsend[p, a - 1, k] = summed(k, to, p).astype(BF16)
            c = remote(xsend.at[p, a - 1], xrecv.at[p, a - 1], xsems.at[p, a - 1], xrsems.at[p, a - 1], at(a, 0)[0])
            c.start()
            x_copies.append(c)
    z_copies = []
    nums = []
    for p in range(parts):
        terms = [summed(k, chip, p) for k in range(count)]
        for a in range(1, chips):
            x_copies[p * (chips - 1) + a - 1].wait_recv()
            terms = [terms[k] + xrecv[p, a - 1, k].astype(F32) for k in range(count)]
        for h, hop in enumerate(HOPS):
            for slot in range(TILE_DEV):
                zsend[p, h, slot] = owed(terms, hop, slot).astype(BF16)
            c = remote(zsend.at[p, h], zrecv.at[p, h], zsems.at[p, h], zrsems.at[p, h], beam(hop))
            c.start()
            z_copies.append(c)
        nums.append([owed(terms, 0, slot) for slot in range(TILE_DEV)])
    for h, c in enumerate(den_copies):
        c.wait_recv()
        dens = [dens[slot] + drecv[h, slot].astype(F32) for slot in range(TILE_DEV)]
    for p in range(parts):
        for h in range(len(HOPS)):
            z_copies[p * len(HOPS) + h].wait_recv()
        for slot in range(TILE_DEV):
            num = nums[p][slot]
            for h in range(len(HOPS)):
                num += zrecv[p, h, slot].astype(F32)
            out_ref[slot, p * cut:(p + 1) * cut] = num / jnp.maximum(dens[slot][p * cut:(p + 1) * cut], 0.5)
    for c in gain_copies + core_copies + den_copies + x_copies + z_copies:
        c.wait_send()


def body(uv_grid, beam_gain, sub_pixel, intersection_tiles, tile_offsets):
    chips, cores = lax.axis_size("fft"), lax.axis_size("sub")
    members = chips * cores
    rows = uv_grid.shape[2]
    length = uv_grid.shape[3]
    own_rows = beam_gain.shape[1]
    window = beam_gain.shape[2]
    side = S // members
    count = tile_offsets.shape[1]
    quarter = RADIX * rows == length
    if quarter:
        row_table = jnp.asarray(row_tables(length, window, rows))
    else:
        member = lax.axis_index("fft") * lax.axis_size("sub") + lax.axis_index("sub")
        freq = member * rows + jnp.arange(rows, dtype=jnp.int32)
        place = jnp.arange(window, dtype=jnp.int32) - window // 2
        angle = jnp.mod(place[:, None] * freq[None, :], length).astype(F32) * (2.0 * np.pi / length)
        row_table = jnp.stack([jnp.cos(angle), jnp.sin(angle)]).astype(BF16)
    col_table = jnp.asarray(column_tables(length, window))
    step = min(128, rows)
    parts = PARTS
    cut = side // parts
    hops = len(HOPS)
    vmem = pl.BlockSpec(memory_space=pltpu.VMEM)
    smem = pl.BlockSpec(memory_space=pltpu.SMEM)
    anywhere = pl.BlockSpec(memory_space=pl.ANY)
    dma = pltpu.SemaphoreType.DMA
    return pl.pallas_call(
        functools.partial(kernel, quarter, step),
        out_shape=jax.ShapeDtypeStruct((TILE_DEV, side, S), F32),
        in_specs=[smem, smem, smem, anywhere, anywhere, anywhere, anywhere],
        out_specs=vmem,
        scratch_shapes=[
            pltpu.VMEM((2, rows, length), F32),
            pltpu.VMEM(col_table.shape, BF16),
            pltpu.VMEM(row_table.shape, BF16),
            pltpu.VMEM((window, 2 * rows), BF16),
            pltpu.VMEM((2 * rows, window), BF16),
            pltpu.VMEM((own_rows, window), F32),
            pltpu.VMEM((window, window), jnp.int16),
            pltpu.VMEM((window // LANES, window, LANES), F32),
            pltpu.VMEM((window // LANES, window, LANES), F32),
            pltpu.VMEM((2, count, window, S), BF16),
            pltpu.VMEM((count, cores, chips, side, S), F32),
            pltpu.VMEM((count, cores, chips, side, S), BF16),
            pltpu.VMEM((cores - 1, count, chips, side, S), BF16),
            pltpu.VMEM((parts, chips - 1, count, cut, S), BF16),
            pltpu.VMEM((parts, chips - 1, count, cut, S), BF16),
            pltpu.VMEM((parts, hops, TILE_DEV, cut, S), BF16),
            pltpu.VMEM((parts, hops, TILE_DEV, cut, S), BF16),
            pltpu.VMEM((hops, TILE_DEV, side, S), BF16),
            pltpu.VMEM((hops, TILE_DEV, side, S), BF16),
            dma((rows // step + 3,)),
            dma((members,)),
            dma((members,)),
            dma((cores - 1, count)),
            dma((cores - 1, count)),
            dma((parts, chips - 1)),
            dma((parts, chips - 1)),
            dma((parts, hops)),
            dma((parts, hops)),
            dma((hops,)),
            dma((hops,)),
        ],
        compiler_params=pltpu.CompilerParams(collective_id=0, has_side_effects=True),
    )(sub_pixel, intersection_tiles, jnp.swapaxes(tile_offsets, 1, 2), beam_gain, uv_grid, col_table, row_table)


def solution(mesh):
    placed = (
        P(("group", "beam"), None, ("fft", "sub"), None),
        P(("group", "beam"), ("fft", "sub"), None),
        P(("group", "beam"), None),
        P("group", None),
        P(("group", "beam"), None, None),
    )
    return jax.shard_map(
        body,
        mesh=mesh,
        in_specs=placed,
        out_specs=P(("group", "beam"), ("fft", "sub"), None),
        check_vma=False,
    )
```

time: 33.1 us -> 32 us (0.967)
  Pallas kernels: 31.3 us -> 30.2 us
    pallas_call x1, Pallas kernels: 31.3 us -> 30.2 us  [body(): pl.pallas_call(functools.partial(kernel, quarter, step), out_shape=jax.Sh...]
where the time goes in v1:
time: 32 us; the launch traced here: 31.8 us
  Pallas kernels  30.2 us (94%)
  local copies, waits for them, and re-layouts  1.57 us (5%)
    pallas_call x1, Pallas kernels, body(): pl.pallas_call(functools.partial(kernel, quarter, step), out_shape=jax.Sh...  30.2 us
    unnamed x1, local copies, waits for them, and re-layouts  1.57 us

profile of v1, /device:TPU:0, one launch (start us, length us, event | category | flops | bytes accessed | tf_op | source)
XLA Modules:
  0.0 31.8 jit_solution(6606543315106124972)
XLA Ops:
  0.0 30.2 %shard_map.73 = f32[2,64,256]{2,1,0:T(8,128)} custom-call(f32[1,2]{1,0:T(1,128)} %shift_ref.1, s32[4,4]{1,0:T(4,128)} %tiles_ref.1, s32[1,2,4]{2,1,0:T(2,128)} %bitcast.1, f32[1,128,512]{2,1,0:T(8,128)} %gain_hbm.1, f32[1,2,512,2048]{3,2,1,0:T(8,128)} %uv_ref.1, bf16[2,4,512,256]{3,2,1,0:T(8,128)(2,1)} %constant.5.clone.col_hbm, ...), custom_call_target="tpu_custom_call" | custom-call | tf_op jit(solution)/shard_map/pallas_call | solution.py:343
  30.2 1.6 %copy.9 = f32[2,64,256]{2,1,0:T(8,128)} copy(f32[2,64,256]{2,1,0:T(8,128)} %shard_map.73) | data formatting | bytes 262144

commit v2 on v1

--- a/solution.py
+++ b/solution.py
@@ -1,4 +1,5 @@
 import functools
+import math
 
 import jax
 import jax.numpy as jnp
@@ -11,7 +12,8 @@
 
 S = 256
 TILE_DEV = 2
-RADIX = 4
+RADIX = 8
+ROOT = math.sqrt(0.5)
 HOPS = (2, 1, -1)
 PARTS = 2
 LEVELS = 32000.0
@@ -32,11 +34,11 @@
     tables = []
     for c in range(RADIX):
         cos, sin = turns(np.arange(fold), RADIX * np.arange(per) + c - window // 2, length)
-        tables.append(np.concatenate([cos, sin], axis=1))
-    full = np.stack(tables).astype(np.float32)
-    high = full.astype(ml_dtypes.bfloat16)
-    low = (full - high.astype(np.float32)).astype(ml_dtypes.bfloat16)
-    return np.stack([high, low])
+        full = np.concatenate([sin, cos] if c % 2 else [cos, sin], axis=1).astype(np.float32)
+        high = full.astype(ml_dtypes.bfloat16)
+        low = (full - high.astype(np.float32)).astype(ml_dtypes.bfloat16)
+        tables.append(np.concatenate([high, low], axis=1))
+    return np.stack(tables)
 
 
 def row_tables(length, window, rows):
@@ -144,61 +146,84 @@
             total += down[d] * pltpu.roll(x, window - d, 0)
         return total
 
-    def rounded(tap):
-        return jnp.full((1, S), tap, F32).astype(BF16).astype(F32)
-
-    tops = [rounded(tap) for tap in across]
-    rests = [tap - top for tap, top in zip(across, tops)]
-    source = natural(place) - lax.broadcasted_iota(jnp.int32, (window, S), 1)
+    def split(tap):
+        tap = jnp.full((1, S), tap, F32)
+        top = tap.astype(BF16)
+        return top, (tap - top.astype(F32)).astype(BF16)
+
+    split_taps = [split(tap) for tap in across]
+    source = (natural(place) - lax.broadcasted_iota(jnp.int32, (window, S), 1)).astype(jnp.int16)
     for k in range(count):
-        gap = source - offs_ref[0, 1, k]
-        top = jnp.zeros((window, S), F32)
+        gap = source - jnp.full((1, S), offs_ref[0, 1, k], jnp.int32).astype(jnp.int16)
+        top = jnp.zeros((window, S), BF16)
         rest = top
         for d in range(4):
             hit = gap == d
-            top = jnp.where(hit, tops[d], top)
-            rest = jnp.where(hit, rests[d], rest)
-        mats[0, k] = top.astype(BF16)
-        mats[1, k] = rest.astype(BF16)
+            top = jnp.where(hit, split_taps[d][0], top)
+            rest = jnp.where(hit, split_taps[d][1], rest)
+        mats[0, k] = top
+        mats[1, k] = rest
+
+    first = lax.broadcasted_iota(jnp.int32, (1, 2 * per), 1) < per
+
+    def quartet(f):
+        (a0, b0), (a1, b1), (a2, b2), (a3, b3) = f
+        ap, am, aq, an = a0 + a2, a0 - a2, a1 + a3, a1 - a3
+        bp, bm, bq, bn = b0 + b2, b0 - b2, b1 + b3, b1 - b3
+        return (ap + aq, bp + bq), (am - bn, bm + an), (ap - aq, bp - bq), (am + bn, bm - an)
 
     def columns(i, carry):
         load(i).wait()
         span = pl.ds(pl.multiple_of(i * step, step), step)
-        a = [buf[0, span, j * fold:(j + 1) * fold] for j in range(RADIX)]
-        b = [buf[1, span, j * fold:(j + 1) * fold] for j in range(RADIX)]
-        ap, am, aq, an = a[0] + a[2], a[0] - a[2], a[1] + a[3], a[1] - a[3]
-        bp, bm, bq, bn = b[0] + b[2], b[0] - b[2], b[1] + b[3], b[1] - b[3]
-        folded = (
-            (ap + aq, bp + bq),
-            (am - bn, bm + an),
-            (ap - aq, bp - bq),
-            (am + bn, bm - an),
-        )
-        for c in range(RADIX):
-            z = jnp.concatenate(folded[c], axis=0)
-            high = z.astype(BF16)
-            low = (z - high.astype(F32)).astype(BF16)
-            out = jnp.dot(high, col_ref[0, c], preferred_element_type=F32)
-            out += jnp.dot(low, col_ref[0, c], preferred_element_type=F32)
-            out += jnp.dot(high, col_ref[1, c], preferred_element_type=F32)
-            real = (out[:step, :per] - out[step:, per:]).astype(BF16)
-            imag = (out[:step, per:] + out[step:, :per]).astype(BF16)
-            spec[span, c * per:(c + 1) * per] = real
-            spec[pl.ds(pl.multiple_of(rows + i * step, step), step), c * per:(c + 1) * per] = imag
+        parts_of = [(buf[0, span, j * fold:(j + 1) * fold], buf[1, span, j * fold:(j + 1) * fold]) for j in range(RADIX)]
+        even, odd = quartet(parts_of[0::2]), quartet(parts_of[1::2])
+        turned = []
+        for c, (x, y) in enumerate(odd):
+            if c == 1:
+                x, y = ROOT * (x - y), ROOT * (x + y)
+            elif c == 2:
+                x, y = -y, x
+            elif c == 3:
+                x, y = -ROOT * (x + y), ROOT * (x - y)
+            turned.append((x, y))
+        folded = [(e[0] + t[0], e[1] + t[1]) for e, t in zip(even, turned)]
+        folded += [(e[0] - t[0], e[1] - t[1]) for e, t in zip(even, turned)]
+        done = pl.ds(pl.multiple_of(rows + i * step, step), step)
+        for c in range(0, RADIX, 2):
+            pair = []
+            for d in range(2):
+                z = jnp.concatenate(folded[c + d], axis=0)
+                high = z.astype(BF16)
+                low = (z - high.astype(F32)).astype(BF16)
+                out = jnp.dot(jnp.concatenate([high, low], axis=0), col_ref[c + d], preferred_element_type=F32)
+                out = out[:2 * step] + out[2 * step:]
+                out = out[:, :2 * per] + out[:, 2 * per:]
+                swapped = pltpu.roll(out[step:], per, 1)
+                pair.append(out[:step] + jnp.where(first, -swapped, swapped) if d == 0
+                            else out[:step] + jnp.where(first, swapped, -swapped))
+            real = jnp.where(first, pair[0], pair[1])
+            imag = pltpu.roll(jnp.where(first, pair[1], pair[0]), per, 1)
+            spec[span, c * per:(c + 2) * per] = real.astype(BF16)
+            spec[done, c * per:(c + 2) * per] = imag.astype(BF16)
         return carry
 
     col_load.wait()
     lax.fori_loop(0, chunks // 2, columns, 0)
     row_load.wait()
-    cos = row_ref[0].astype(F32)
-    sin = row_ref[1].astype(F32)
+    cos, sin = row_ref[0], row_ref[1]
     if quarter:
         turn = jnp.bitwise_and(me * place, 3)
         plus = jnp.where(turn == 0, 1.0, jnp.where(turn == 2, -1.0, 0.0))
         cross = jnp.where(turn == 1, 1.0, jnp.where(turn == 3, -1.0, 0.0))
-        cos, sin = plus * cos - cross * sin, cross * cos + plus * sin
-    table[:, :rows] = cos.astype(BF16)
-    table[:, rows:] = (-sin).astype(BF16)
+        plus = jnp.broadcast_to(plus, (window, LANES)).astype(BF16)
+        cross = jnp.broadcast_to(cross, (window, LANES)).astype(BF16)
+        for q in range(rows // LANES):
+            x, y = cos[:, q * LANES:(q + 1) * LANES], sin[:, q * LANES:(q + 1) * LANES]
+            table[:, q * LANES:(q + 1) * LANES] = plus * x - cross * y
+            table[:, rows + q * LANES:rows + (q + 1) * LANES] = -(cross * x + plus * y)
+    else:
+        table[:, :rows] = cos
+        table[:, rows:] = -sin
     lax.fori_loop(chunks // 2, chunks - 1, columns, 0)
     for a in range(1, chips):
         frm = at(-a, 0)[1]
@@ -322,7 +347,7 @@
     window = beam_gain.shape[2]
     side = S // members
     count = tile_offsets.shape[1]
-    quarter = RADIX * rows == length
+    quarter = 4 * rows == length
     if quarter:
         row_table = jnp.asarray(row_tables(length, window, rows))
     else:

time: 32 us -> 31.3 us (0.978)
  Pallas kernels: 30.2 us -> 29.6 us
    pallas_call x1, Pallas kernels: 30.2 us -> 29.6 us  [body(): pl.pallas_call(functools.partial(kernel, quarter, step), out_shape=jax.Sh...]
where the time goes in v2:
time: 31.3 us; the launch traced here: 31.2 us
  Pallas kernels  29.6 us (95%)
  local copies, waits for them, and re-layouts  1.57 us (5%)
    pallas_call x1, Pallas kernels, body(): pl.pallas_call(functools.partial(kernel, quarter, step), out_shape=jax.Sh...  29.6 us
    unnamed x1, local copies, waits for them, and re-layouts  1.57 us

profile of v2, /device:TPU:0, one launch (start us, length us, event | category | flops | bytes accessed | tf_op | source)
XLA Modules:
  0.0 31.2 jit_solution(10143578869980348006)
XLA Ops:
  0.0 29.6 %shard_map.73 = f32[2,64,256]{2,1,0:T(8,128)} custom-call(f32[1,2]{1,0:T(1,128)} %shift_ref.1, s32[4,4]{1,0:T(4,128)} %tiles_ref.1, s32[1,2,4]{2,1,0:T(2,128)} %bitcast.1, f32[1,128,512]{2,1,0:T(8,128)} %gain_hbm.1, f32[1,2,512,2048]{3,2,1,0:T(8,128)} %uv_ref.1, bf16[8,256,256]{2,1,0:T(8,128)(2,1)} %constant.5.clone.col_hbm, ...), custom_call_target="tpu_custom_call" | custom-call | tf_op jit(solution)/shard_map/pallas_call | solution.py:368
  29.6 1.6 %copy.9 = f32[2,64,256]{2,1,0:T(8,128)} copy(f32[2,64,256]{2,1,0:T(8,128)} %shard_map.73) | data formatting | bytes 262144

commit v3 on v2

--- a/solution.py
+++ b/solution.py
@@ -15,9 +15,10 @@
 RADIX = 8
 ROOT = math.sqrt(0.5)
 HOPS = (2, 1, -1)
-PARTS = 2
+PARTS = 1
 LEVELS = 32000.0
 LANES = 128
+PACK = 16
 MESH = pl.DeviceIdType.MESH
 F32 = jnp.float32
 BF16 = jnp.bfloat16
@@ -60,7 +61,7 @@
 
 def kernel(
     quarter, step, shift_ref, tiles_ref, offs_ref, gain_hbm, uv_ref, col_hbm, row_hbm, out_ref,
-    buf, col_ref, row_ref, table, spec, own, gall, filt, squares, mats, pieces, psend, precv,
+    buf, zbuf, col_ref, row_ref, table, spec, own, gall, filt, squares, mats, pieces, psend, precv,
     xsend, xrecv, zsend, zrecv, dsend, drecv,
     load_sems, gsems, grecv, csems, crecv, xsems, xrsems, zsems, zrsems, dsems, drsems,
 ):
@@ -172,67 +173,84 @@
         bp, bm, bq, bn = b0 + b2, b0 - b2, b1 + b3, b1 - b3
         return (ap + aq, bp + bq), (am - bn, bm + an), (ap - aq, bp - bq), (am + bn, bm - an)
 
-    def columns(i, carry):
-        load(i).wait()
-        span = pl.ds(pl.multiple_of(i * step, step), step)
-        parts_of = [(buf[0, span, j * fold:(j + 1) * fold], buf[1, span, j * fold:(j + 1) * fold]) for j in range(RADIX)]
-        even, odd = quartet(parts_of[0::2]), quartet(parts_of[1::2])
-        turned = []
-        for c, (x, y) in enumerate(odd):
-            if c == 1:
-                x, y = ROOT * (x - y), ROOT * (x + y)
-            elif c == 2:
-                x, y = -y, x
-            elif c == 3:
-                x, y = -ROOT * (x + y), ROOT * (x - y)
-            turned.append((x, y))
-        folded = [(e[0] + t[0], e[1] + t[1]) for e, t in zip(even, turned)]
-        folded += [(e[0] - t[0], e[1] - t[1]) for e, t in zip(even, turned)]
-        done = pl.ds(pl.multiple_of(rows + i * step, step), step)
+    def lanes_of(ref):
+        return jnp.concatenate([ref[t] for t in range(ref.shape[0])], axis=1)
+
+    def fold_rows(i, start, stop):
+        for r in range(start, stop, PACK):
+            for t in range(0, fold, LANES):
+                span = slice(i * step + r, i * step + r + PACK)
+                pieces_of = [tuple(buf[n, span, j * fold + t:j * fold + t + LANES] for n in range(2)) for j in range(RADIX)]
+                even, odd = quartet(pieces_of[0::2]), quartet(pieces_of[1::2])
+                for c in range(RADIX // 2):
+                    x, y = odd[c]
+                    if c == 1:
+                        x, y = ROOT * (x - y), ROOT * (x + y)
+                    elif c == 2:
+                        x, y = -y, x
+                    elif c == 3:
+                        x, y = -ROOT * (x + y), ROOT * (x - y)
+                    e, f = even[c]
+                    for d, z in ((c, (e + x, f + y)), (c + RADIX // 2, (e - x, f - y))):
+                        for n in range(2):
+                            high = z[n].astype(BF16)
+                            zbuf[i % 2, d, 0, t // LANES, n * step + r:n * step + r + PACK] = high
+                            zbuf[i % 2, d, 1, t // LANES, n * step + r:n * step + r + PACK] = (
+                                z[n] - high.astype(F32)).astype(BF16)
+
+    def transform(i):
         for c in range(0, RADIX, 2):
+            if i + 1 < chunks:
+                fold_rows(i + 1, c * step // RADIX, (c + 2) * step // RADIX)
             pair = []
             for d in range(2):
-                z = jnp.concatenate(folded[c + d], axis=0)
-                high = z.astype(BF16)
-                low = (z - high.astype(F32)).astype(BF16)
-                out = jnp.dot(jnp.concatenate([high, low], axis=0), col_ref[c + d], preferred_element_type=F32)
-                out = out[:2 * step] + out[2 * step:]
+                out = jnp.dot(lanes_of(zbuf.at[i % 2, c + d, 0]), col_ref[c + d], preferred_element_type=F32)
+                out += jnp.dot(lanes_of(zbuf.at[i % 2, c + d, 1]), col_ref[c + d], preferred_element_type=F32)
                 out = out[:, :2 * per] + out[:, 2 * per:]
                 swapped = pltpu.roll(out[step:], per, 1)
                 pair.append(out[:step] + jnp.where(first, -swapped, swapped) if d == 0
                             else out[:step] + jnp.where(first, swapped, -swapped))
             real = jnp.where(first, pair[0], pair[1])
             imag = pltpu.roll(jnp.where(first, pair[1], pair[0]), per, 1)
-            spec[span, c * per:(c + 2) * per] = real.astype(BF16)
-            spec[done, c * per:(c + 2) * per] = imag.astype(BF16)
-        return carry
-
+            spec[i * step:(i + 1) * step, c * per:(c + 2) * per] = real.astype(BF16)
+            spec[rows + i * step:rows + (i + 1) * step, c * per:(c + 2) * per] = imag.astype(BF16)
+
+    def forward():
+        for a in range(1, chips):
+            frm = at(-a, 0)[1]
+            gain_copy(a, 0, frm).wait_recv()
+            for e in range(1, cores):
+                c = gain_copy(a, e, frm)
+                c.start()
+                gain_copies.append(c)
+
+    def make_table():
+        row_load.wait()
+        cos, sin = row_ref[0], row_ref[1]
+        if quarter:
+            turn = jnp.bitwise_and(me * place, 3)
+            plus = jnp.where(turn == 0, 1.0, jnp.where(turn == 2, -1.0, 0.0))
+            cross = jnp.where(turn == 1, 1.0, jnp.where(turn == 3, -1.0, 0.0))
+            plus = jnp.broadcast_to(plus, (window, LANES)).astype(BF16)
+            cross = jnp.broadcast_to(cross, (window, LANES)).astype(BF16)
+            for q in range(rows // LANES):
+                x, y = cos[:, q * LANES:(q + 1) * LANES], sin[:, q * LANES:(q + 1) * LANES]
+                table[:, q * LANES:(q + 1) * LANES] = plus * x - cross * y
+                table[:, rows + q * LANES:rows + (q + 1) * LANES] = -(cross * x + plus * y)
+        else:
+            table[:, :rows] = cos
+            table[:, rows:] = -sin
+
+    load(0).wait()
+    fold_rows(0, 0, step)
     col_load.wait()
-    lax.fori_loop(0, chunks // 2, columns, 0)
-    row_load.wait()
-    cos, sin = row_ref[0], row_ref[1]
-    if quarter:
-        turn = jnp.bitwise_and(me * place, 3)
-        plus = jnp.where(turn == 0, 1.0, jnp.where(turn == 2, -1.0, 0.0))
-        cross = jnp.where(turn == 1, 1.0, jnp.where(turn == 3, -1.0, 0.0))
-        plus = jnp.broadcast_to(plus, (window, LANES)).astype(BF16)
-        cross = jnp.broadcast_to(cross, (window, LANES)).astype(BF16)
-        for q in range(rows // LANES):
-            x, y = cos[:, q * LANES:(q + 1) * LANES], sin[:, q * LANES:(q + 1) * LANES]
-            table[:, q * LANES:(q + 1) * LANES] = plus * x - cross * y
-            table[:, rows + q * LANES:rows + (q + 1) * LANES] = -(cross * x + plus * y)
-    else:
-        table[:, :rows] = cos
-        table[:, rows:] = -sin
-    lax.fori_loop(chunks // 2, chunks - 1, columns, 0)
-    for a in range(1, chips):
-        frm = at(-a, 0)[1]
-        gain_copy(a, 0, frm).wait_recv()
-        for e in range(1, cores):
-            c = gain_copy(a, e, frm)
-            c.start()
-            gain_copies.append(c)
-    lax.fori_loop(chunks - 1, chunks, columns, 0)
+    for i in range(chunks):
+        if i + 1 < chunks:
+            load(i + 1).wait()
+        transform(i)
+        if i == chunks - 2:
+            make_table()
+            forward()
 
     for a in range(chips):
         for e in range(1, cores):
@@ -372,6 +390,7 @@
         out_specs=vmem,
         scratch_shapes=[
             pltpu.VMEM((2, rows, length), F32),
+            pltpu.VMEM((2, RADIX, 2, length // RADIX // LANES, 2 * step, LANES), BF16),
             pltpu.VMEM(col_table.shape, BF16),
             pltpu.VMEM(row_table.shape, BF16),
             pltpu.VMEM((window, 2 * rows), BF16),

time: 31.3 us -> 30.9 us (0.987)
  Pallas kernels: 29.6 us -> 29.1 us
    pallas_call x1, Pallas kernels: 29.6 us -> 29.1 us  [body(): pl.pallas_call(functools.partial(kernel, quarter, step), out_shape=jax.Sh...]
where the time goes in v3:
time: 30.9 us; the launch traced here: 30.7 us
  Pallas kernels  29.1 us (94%)
  local copies, waits for them, and re-layouts  1.57 us (5%)
    pallas_call x1, Pallas kernels, body(): pl.pallas_call(functools.partial(kernel, quarter, step), out_shape=jax.Sh...  29.1 us
    unnamed x1, local copies, waits for them, and re-layouts  1.57 us

profile of v3, /device:TPU:0, one launch (start us, length us, event | category | flops | bytes accessed | tf_op | source)
XLA Modules:
  0.0 30.7 jit_solution(8521869421978191950)
XLA Ops:
  0.0 29.1 %shard_map.73 = f32[2,64,256]{2,1,0:T(8,128)} custom-call(f32[1,2]{1,0:T(1,128)} %shift_ref.1, s32[4,4]{1,0:T(4,128)} %tiles_ref.1, s32[1,2,4]{2,1,0:T(2,128)} %bitcast.1, f32[1,128,512]{2,1,0:T(8,128)} %gain_hbm.1, f32[1,2,512,2048]{3,2,1,0:T(8,128)} %uv_ref.1, bf16[8,256,256]{2,1,0:T(8,128)(2,1)} %constant.5.clone.col_hbm, ...), custom_call_target="tpu_custom_call" | custom-call | tf_op jit(solution)/shard_map/pallas_call | solution.py:386
  29.1 1.6 %copy.9 = f32[2,64,256]{2,1,0:T(8,128)} copy(f32[2,64,256]{2,1,0:T(8,128)} %shard_map.73) | data formatting | bytes 262144

commit v4 on v3

--- a/solution.py
+++ b/solution.py
@@ -60,8 +60,8 @@
 
 
 def kernel(
-    quarter, step, shift_ref, tiles_ref, offs_ref, gain_hbm, uv_ref, col_hbm, row_hbm, out_ref,
-    buf, zbuf, col_ref, row_ref, table, spec, own, gall, filt, squares, mats, pieces, psend, precv,
+    quarter, step, shift_hbm, tiles_hbm, offs_hbm, gain_hbm, uv_ref, col_hbm, row_hbm, out_ref,
+    shift_ref, tiles_ref, offs_ref, buf, zbuf, col_ref, row_ref, table, spec, own, gall, filt, squares, mats, pieces, psend, precv,
     xsend, xrecv, zsend, zrecv, dsend, drecv,
     load_sems, gsems, grecv, csems, crecv, xsems, xrsems, zsems, zrsems, dsems, drsems,
 ):
@@ -87,7 +87,12 @@
     gain_load = pltpu.make_async_copy(gain_hbm.at[0], own, load_sems.at[chunks])
     col_load = pltpu.make_async_copy(col_hbm, col_ref, load_sems.at[chunks + 1])
     row_load = pltpu.make_async_copy(row_hbm, row_ref, load_sems.at[chunks + 2])
+    small_loads = [
+        pltpu.make_async_copy(src, dst, load_sems.at[chunks + 3 + n])
+        for n, (src, dst) in enumerate(((shift_hbm, shift_ref), (tiles_hbm, tiles_ref), (offs_hbm, offs_ref)))]
     gain_load.start()
+    for c in small_loads:
+        c.start()
     col_load.start()
     for i in range(chunks):
         load(i).start()
@@ -138,6 +143,8 @@
     for c in gain_copies:
         c.start()
 
+    for c in small_loads:
+        c.wait()
     down = taps(shift_ref[0, 0])
     across = taps(shift_ref[0, 1])
 
@@ -275,12 +282,12 @@
             for e in range(cores):
                 m = a * cores + e
                 pieces[k, e, a] = piece[m * side:(m + 1) * side]
-                psend[k, e, a] = piece[m * side:(m + 1) * side].astype(BF16)
-        for e in range(1, cores):
-            to = lax.rem(core + e, cores)
-            c = remote(psend.at[k, to], precv.at[e - 1, k], csems.at[e - 1, k], crecv.at[e - 1, k], at(0, e)[0])
-            c.start()
-            core_copies.append(c)
+                psend[e, k, a] = piece[m * side:(m + 1) * side].astype(BF16)
+    for e in range(1, cores):
+        to = lax.rem(core + e, cores)
+        c = remote(psend.at[to], precv.at[e - 1], csems.at[e - 1], crecv.at[e - 1], at(0, e)[0])
+        c.start()
+        core_copies.append(c)
 
     def owed(terms, hop, slot):
         tile = lax.rem(owner + hop + owners, owners) * TILE_DEV + slot
@@ -380,15 +387,17 @@
     cut = side // parts
     hops = len(HOPS)
     vmem = pl.BlockSpec(memory_space=pltpu.VMEM)
-    smem = pl.BlockSpec(memory_space=pltpu.SMEM)
     anywhere = pl.BlockSpec(memory_space=pl.ANY)
     dma = pltpu.SemaphoreType.DMA
     return pl.pallas_call(
         functools.partial(kernel, quarter, step),
         out_shape=jax.ShapeDtypeStruct((TILE_DEV, side, S), F32),
-        in_specs=[smem, smem, smem, anywhere, anywhere, anywhere, anywhere],
+        in_specs=[anywhere] * 7,
         out_specs=vmem,
         scratch_shapes=[
+            pltpu.SMEM(sub_pixel.shape, F32),
+            pltpu.SMEM(intersection_tiles.shape, jnp.int32),
+            pltpu.SMEM((1, 2, count), jnp.int32),
             pltpu.VMEM((2, rows, length), F32),
             pltpu.VMEM((2, RADIX, 2, length // RADIX // LANES, 2 * step, LANES), BF16),
             pltpu.VMEM(col_table.shape, BF16),
@@ -401,7 +410,7 @@
             pltpu.VMEM((window // LANES, window, LANES), F32),
             pltpu.VMEM((2, count, window, S), BF16),
             pltpu.VMEM((count, cores, chips, side, S), F32),
-            pltpu.VMEM((count, cores, chips, side, S), BF16),
+            pltpu.VMEM((cores, count, chips, side, S), BF16),
             pltpu.VMEM((cores - 1, count, chips, side, S), BF16),
             pltpu.VMEM((parts, chips - 1, count, cut, S), BF16),
             pltpu.VMEM((parts, chips - 1, count, cut, S), BF16),
@@ -409,11 +418,11 @@
             pltpu.VMEM((parts, hops, TILE_DEV, cut, S), BF16),
             pltpu.VMEM((hops, TILE_DEV, side, S), BF16),
             pltpu.VMEM((hops, TILE_DEV, side, S), BF16),
-            dma((rows // step + 3,)),
+            dma((rows // step + 6,)),
             dma((members,)),
             dma((members,)),
-            dma((cores - 1, count)),
-            dma((cores - 1, count)),
+            dma((cores - 1,)),
+            dma((cores - 1,)),
             dma((parts, chips - 1)),
             dma((parts, chips - 1)),
             dma((parts, hops)),

time: 30.9 us -> 29.2 us (0.945)
  Pallas kernels: 29.1 us -> 27.5 us
    pallas_call x1, Pallas kernels: 29.1 us -> 27.5 us  [body(): pl.pallas_call(functools.partial(kernel, quarter, step), out_shape=jax.Sh...]
where the time goes in v4:
time: 29.2 us; the launch traced here: 29.1 us
  Pallas kernels  27.5 us (94%)
  local copies, waits for them, and re-layouts  1.57 us (5%)
    pallas_call x1, Pallas kernels, body(): pl.pallas_call(functools.partial(kernel, quarter, step), out_shape=jax.Sh...  27.5 us
    unnamed x1, local copies, waits for them, and re-layouts  1.57 us

profile of v4, /device:TPU:0, one launch (start us, length us, event | category | flops | bytes accessed | tf_op | source)
XLA Modules:
  0.0 29.1 jit_solution(2722799551255227855)
XLA Ops:
  0.0 27.5 %shard_map.73 = f32[2,64,256]{2,1,0:T(8,128)} custom-call(f32[1,2]{1,0:T(1,128)} %shift_hbm.1, s32[4,4]{1,0:T(4,128)} %tiles_hbm.1, s32[1,2,4]{2,1,0:T(2,128)} %bitcast.1, f32[1,128,512]{2,1,0:T(8,128)} %gain_hbm.1, f32[1,2,512,2048]{3,2,1,0:T(8,128)} %uv_ref.1, bf16[8,256,256]{2,1,0:T(8,128)(2,1)} %constant.5.clone.col_hbm, ...), custom_call_target="tpu_custom_call" | custom-call | tf_op jit(solution)/shard_map/pallas_call | solution.py:392
  27.5 1.6 %copy.9 = f32[2,64,256]{2,1,0:T(8,128)} copy(f32[2,64,256]{2,1,0:T(8,128)} %shard_map.73) | data formatting | bytes 262144
